TPU v7x, 32 devices: a whole 2x2x4 slice. The times are simulated.
32 devices in a mesh: vid: 2 (over core), txt: 4 (over y, x), head: 4 (over z).
Axes of the slice: x: 2, y: 2, z: 4, core: 2. Of those that a mesh axis runs over, the one named last changes fastest.
Arguments:
- latents: bfloat16 [32, 128, 768], P('txt', 'vid'), may hold values from -6 to 6
- video_tokens: bfloat16 [32, 1024, 768], P('txt', 'vid'), may hold values from -6 to 6
- caption_tokens: bfloat16 [32, 64, 768], P('vid', 'txt'), may hold values from -6 to 6
- caption_len: int32 [32], P('vid'), may hold values from 5 to 60
- key_mask: int32 [32, 64], P('vid', 'txt'), may hold values 0 or 1
- drop_flags: int32 [32], P('txt'), may hold values 0 or 1
- gain_latent: float32 [768], replicated, may hold values from 0.5 to 1.5
- gain_tokens: float32 [768], replicated, may hold values from 0.5 to 1.5
- gain_mlp: float32 [768], replicated, may hold values from 0.5 to 1.5
- query_weight: bfloat16 [768, 768], P(None, 'head'), may hold values from -0.21875 to 0.21875
- key_matrix: bfloat16 [768, 768], P(None, 'head'), may hold values from -0.21875 to 0.21875
- value_matrix: bfloat16 [768, 768], P(None, 'head'), may hold values from -0.21875 to 0.21875
- out_weight: bfloat16 [768, 768], P('head'), may hold values from -6 to 6
- up_weight: bfloat16 [768, 3072], P(None, 'head'), may hold values from -0.21875 to 0.21875
- down_weight: bfloat16 [3072, 768], P('head'), may hold values from -0.109375 to 0.109375
- cotangent: bfloat16 [32, 128, 768], P('txt', 'vid'), may hold values from -6 to 6
Outputs:
- latents_out: bfloat16 [32, 128, 768], P('txt', 'vid')
- latent_grad: float32 [32, 128, 768], P('txt', 'vid')
- video_grad: float32 [32, 1024, 768], P('txt', 'vid')
- caption_grad: float32 [32, 64, 768], P('vid', 'txt')
- grad_query: float32 [768, 768], P(None, 'head')
- grad_key: float32 [768, 768], P(None, 'head')
- grad_value: float32 [768, 768], P(None, 'head')
- grad_out: float32 [768, 768], P('head')
- grad_up: float32 [768, 3072], P(None, 'head')
- grad_down: float32 [3072, 768], P('head')
- grad_gain_latent: float32 [768], replicated
- grad_gain_tokens: float32 [768], replicated
- grad_gain_mlp: float32 [768], replicated
- kept_count: int32 [], replicated
All inputs are finite; a program needn't handle non-finite values. No bound on the sum of `key_mask` or of `drop_flags` on one device may be relied on, other than what follows from the above.
Results may differ from a plain program's by a relative error of at most 0.012.
Values may be sent and summed in bfloat16 or wider, within the bound.
No kernel may reach another device: no remote copies, remote signals or barrier semaphores. Data moves between devices by JAX's collectives and lax.ppermute only.
A program may use at most 128 MiB of HBM per device.

v0:
```python
import math
import jax
import jax.numpy as jnp
from jax import lax
from jax.sharding import PartitionSpec as P

D = 768
HEADS = 12


def combined_all(part, axis, combine):
    gathered = jax.tree.map(lambda a: lax.all_gather(a, axis), part)

    def take(source):
        return jax.tree.map(lambda a: lax.dynamic_index_in_dim(a, source, 0, False), gathered)

    return lax.fori_loop(
        1, lax.axis_size(axis), lambda source, state: combine(state, take(source)), take(0)
    )


def layer_norm(values, gain):
    center = values - jnp.mean(values, axis=-1, keepdims=True)
    spread = jnp.mean(center * center, axis=-1, keepdims=True)
    return center * lax.rsqrt(spread + 1e-05) * gain


def norm_back(values, gain, upstream):
    result, pullback = jax.vjp(layer_norm, values, gain)
    return pullback(upstream)


def gelu_exact(values):
    return jax.nn.gelu(values, approximate=False)


def combine_stats(first, second):
    peak = jnp.maximum(first[0], second[0])
    total = first[1] * jnp.exp(first[0] - peak) + second[1] * jnp.exp(second[0] - peak)
    return (peak, total)


def to_blocks(whole, vid_count, txt_count):
    items, rows, width = whole.shape
    split = whole.reshape(txt_count, items // txt_count, vid_count, rows // vid_count, width)
    return split.transpose(2, 0, 1, 3, 4).reshape(
        vid_count * txt_count, items // txt_count, rows // vid_count, width
    )


def from_blocks(blocked, vid_count, txt_count):
    count, items_here, rows_here, width = blocked.shape
    split = blocked.reshape(vid_count, txt_count, items_here, rows_here, width)
    return split.transpose(1, 2, 0, 3, 4).reshape(
        txt_count * items_here, vid_count * rows_here, width
    )


def place_sum(whole, part, start):
    current = lax.dynamic_slice_in_dim(whole, start, part.shape[0], 0)
    return lax.dynamic_update_slice_in_dim(whole, current + part, start, 0)


def place_stats(peak_all, total_all, peak, total, start):
    old_peak = lax.dynamic_slice_in_dim(peak_all, start, peak.shape[0], 0)
    old_total = lax.dynamic_slice_in_dim(total_all, start, peak.shape[0], 0)
    new_peak, new_total = combine_stats((old_peak, old_total), (peak, total))
    peak_all = lax.dynamic_update_slice_in_dim(peak_all, new_peak, start, 0)
    total_all = lax.dynamic_update_slice_in_dim(total_all, new_total, start, 0)
    return (peak_all, total_all)


def take_rows(whole, start, count):
    return lax.dynamic_slice_in_dim(whole, start, count, 0)


def local(
    latents,
    video_tokens,
    caption_tokens,
    caption_len,
    key_mask,
    drop_flags,
    gain_latent,
    gain_tokens,
    gain_mlp,
    query_weight,
    key_matrix,
    value_matrix,
    out_weight,
    up_weight,
    down_weight,
    cotangent,
):
    vid_count = lax.axis_size("vid")
    txt_count = lax.axis_size("txt")
    vid_index = lax.axis_index("vid")
    txt_index = lax.axis_index("txt")
    items_here = latents.shape[0]
    cap_items = caption_tokens.shape[0]
    items_total = items_here * txt_count
    head_width = query_weight.shape[1]
    head_size = D // HEADS
    heads_here = head_width // head_size
    scale = 1.0 / math.sqrt(head_size)
    video_here = video_tokens.shape[1]
    cap_here = caption_tokens.shape[1]
    video_start = txt_index * items_here
    cap_start = vid_index * cap_items
    keep = (1 - drop_flags).astype(jnp.float32)
    slots = txt_index * cap_here + jnp.arange(cap_here, dtype=jnp.int32)
    cap_valid = (slots[None, :] < caption_len[:, None]) & (key_mask == 1)
    cap_mask = cap_valid[:, None, None, :]

    def split_heads(values):
        return values.reshape(values.shape[0], values.shape[1], heads_here, head_size)

    lat_float = latents.astype(jnp.float32)
    lat_norm = layer_norm(lat_float, gain_latent).astype(jnp.bfloat16)
    queries = jnp.einsum(
        "bld,de->ble", lat_norm, query_weight, preferred_element_type=jnp.float32
    ).astype(jnp.bfloat16)
    all_queries = from_blocks(
        lax.all_gather(queries[None], ("vid", "txt"), axis=0, tiled=True), vid_count, txt_count
    )
    lat_total = all_queries.shape[1]
    video_queries = take_rows(all_queries, video_start, items_here)
    cap_queries = take_rows(all_queries, cap_start, cap_items)
    video_float = video_tokens.astype(jnp.float32)
    cap_float = caption_tokens.astype(jnp.float32)
    video_normed = layer_norm(video_float, gain_tokens).astype(jnp.bfloat16)
    caption_normed = layer_norm(cap_float, gain_tokens).astype(jnp.bfloat16)
    video_keys = jnp.einsum(
        "flc,co->flo", video_normed, key_matrix, preferred_element_type=jnp.float32
    ).astype(jnp.bfloat16)
    video_values = jnp.einsum(
        "flc,co->flo", video_normed, value_matrix, preferred_element_type=jnp.float32
    ).astype(jnp.bfloat16)
    cap_keys = jnp.einsum(
        "flc,co->flo", caption_normed, key_matrix, preferred_element_type=jnp.float32
    ).astype(jnp.bfloat16)
    cap_values = jnp.einsum(
        "flc,co->flo", caption_normed, value_matrix, preferred_element_type=jnp.float32
    ).astype(jnp.bfloat16)
    video_scores = (
        jnp.einsum(
            "blhe,bkhe->bhlk",
            split_heads(video_queries),
            split_heads(video_keys),
            preferred_element_type=jnp.float32,
        )
        * scale
    )
    cap_scores = (
        jnp.einsum(
            "blhe,bkhe->bhlk",
            split_heads(cap_queries),
            split_heads(cap_keys),
            preferred_element_type=jnp.float32,
        )
        * scale
    )
    cap_scores = jnp.where(cap_mask, cap_scores, -1e30)
    video_peak = jnp.max(video_scores, axis=-1)
    video_total = jnp.sum(jnp.exp(video_scores - video_peak[..., None]), axis=-1)
    cap_peak = jnp.max(cap_scores, axis=-1)
    cap_total = jnp.sum(
        jnp.where(cap_mask, jnp.exp(cap_scores - cap_peak[..., None]), 0.0), axis=-1
    )
    peak_all = jnp.full((items_total, heads_here, lat_total), -1e30, jnp.float32)
    total_all = jnp.zeros((items_total, heads_here, lat_total), jnp.float32)
    peak_all, total_all = place_stats(peak_all, total_all, video_peak, video_total, video_start)
    peak_all, total_all = place_stats(peak_all, total_all, cap_peak, cap_total, cap_start)
    peak, total = combined_all((peak_all, total_all), ("vid", "txt"), combine_stats)
    video_probs = (
        jnp.exp(video_scores - take_rows(peak, video_start, items_here)[..., None])
        / take_rows(total, video_start, items_here)[..., None]
    )
    cap_probs = jnp.where(
        cap_mask,
        jnp.exp(cap_scores - take_rows(peak, cap_start, cap_items)[..., None])
        / take_rows(total, cap_start, cap_items)[..., None],
        0.0,
    )
    video_low = video_probs.astype(jnp.bfloat16)
    cap_low = cap_probs.astype(jnp.bfloat16)
    video_part = jnp.einsum(
        "bhlk,bkhe->blhe", video_low, split_heads(video_values), preferred_element_type=jnp.float32
    ).reshape(items_here, lat_total, head_width)
    cap_part = jnp.einsum(
        "bhlk,bkhe->blhe", cap_low, split_heads(cap_values), preferred_element_type=jnp.float32
    ).reshape(cap_items, lat_total, head_width)
    value_all = jnp.zeros((items_total, lat_total, head_width), jnp.float32)
    value_all = place_sum(place_sum(value_all, video_part, video_start), cap_part, cap_start)
    attended = lax.psum_scatter(
        to_blocks(value_all, vid_count, txt_count), ("vid", "txt"), scatter_dimension=0, tiled=True
    )[0]
    mixed_in = (attended * keep[:, None, None]).astype(jnp.bfloat16)
    branch = lax.psum(
        jnp.einsum("ble,ed->bld", mixed_in, out_weight, preferred_element_type=jnp.float32), "head"
    )
    after_attn = lat_float + branch
    mlp_norm = layer_norm(after_attn, gain_mlp).astype(jnp.bfloat16)
    pre_act = jnp.einsum("bld,df->blf", mlp_norm, up_weight, preferred_element_type=jnp.float32)
    activ = gelu_exact(pre_act).astype(jnp.bfloat16)
    growth = lax.psum(
        jnp.einsum("blf,fd->bld", activ, down_weight, preferred_element_type=jnp.float32).astype(
            jnp.bfloat16
        ),
        "head",
    ).astype(jnp.float32)
    latents_out = (after_attn + growth).astype(jnp.bfloat16)
    grad_down = jnp.einsum("blf,bld->fd", activ, cotangent, preferred_element_type=jnp.float32)
    d_activ = jnp.einsum("bld,fd->blf", cotangent, down_weight, preferred_element_type=jnp.float32)
    d_pre = jax.vjp(gelu_exact, pre_act)[1](d_activ)[0].astype(jnp.bfloat16)
    grad_up = jnp.einsum("bld,blf->df", mlp_norm, d_pre, preferred_element_type=jnp.float32)
    d_mlp_norm = lax.psum(
        jnp.einsum("blf,df->bld", d_pre, up_weight, preferred_element_type=jnp.float32), "head"
    )
    d_after_norm, grad_gain_mlp = norm_back(after_attn, gain_mlp, d_mlp_norm)
    d_after = cotangent.astype(jnp.float32) + d_after_norm
    d_branch = d_after.astype(jnp.bfloat16)
    grad_out = jnp.einsum("ble,bld->ed", mixed_in, d_branch, preferred_element_type=jnp.float32)
    d_att = (
        jnp.einsum("bld,ed->ble", d_branch, out_weight, preferred_element_type=jnp.float32)
        * keep[:, None, None]
    ).astype(jnp.bfloat16)
    all_d_att = from_blocks(
        lax.all_gather(d_att[None], ("vid", "txt"), axis=0, tiled=True), vid_count, txt_count
    )
    video_d_att = split_heads(take_rows(all_d_att, video_start, items_here))
    cap_d_att = split_heads(take_rows(all_d_att, cap_start, cap_items))
    video_dprobs = jnp.einsum(
        "blhe,bkhe->bhlk",
        video_d_att,
        split_heads(video_values),
        preferred_element_type=jnp.float32,
    )
    cap_dprobs = jnp.einsum(
        "blhe,bkhe->bhlk", cap_d_att, split_heads(cap_values), preferred_element_type=jnp.float32
    )
    delta_all = jnp.zeros((items_total, heads_here, lat_total), jnp.float32)
    delta_all = place_sum(delta_all, jnp.sum(video_probs * video_dprobs, axis=-1), video_start)
    delta_all = place_sum(delta_all, jnp.sum(cap_probs * cap_dprobs, axis=-1), cap_start)
    delta = lax.psum(delta_all, ("vid", "txt"))
    video_dscores = (
        video_probs * (video_dprobs - take_rows(delta, video_start, items_here)[..., None])
    ).astype(jnp.bfloat16)
    cap_dscores = (
        cap_probs * (cap_dprobs - take_rows(delta, cap_start, cap_items)[..., None])
    ).astype(jnp.bfloat16)
    video_dq = (
        jnp.einsum(
            "bhlk,bkhe->blhe",
            video_dscores,
            split_heads(video_keys),
            preferred_element_type=jnp.float32,
        )
        * scale
    ).reshape(items_here, lat_total, head_width)
    cap_dq = (
        jnp.einsum(
            "bhlk,bkhe->blhe",
            cap_dscores,
            split_heads(cap_keys),
            preferred_element_type=jnp.float32,
        )
        * scale
    ).reshape(cap_items, lat_total, head_width)
    query_all = jnp.zeros((items_total, lat_total, head_width), jnp.float32)
    query_all = place_sum(place_sum(query_all, video_dq, video_start), cap_dq, cap_start)
    d_queries = lax.psum_scatter(
        to_blocks(query_all, vid_count, txt_count), ("vid", "txt"), scatter_dimension=0, tiled=True
    )[0].astype(jnp.bfloat16)
    video_key_grad = (
        (
            jnp.einsum(
                "bhlk,blhe->bkhe",
                video_dscores,
                split_heads(video_queries),
                preferred_element_type=jnp.float32,
            )
            * scale
        )
        .reshape(items_here, video_here, head_width)
        .astype(jnp.bfloat16)
    )
    video_value_grad = (
        jnp.einsum("bhlk,blhe->bkhe", video_low, video_d_att, preferred_element_type=jnp.float32)
        .reshape(items_here, video_here, head_width)
        .astype(jnp.bfloat16)
    )
    caption_key_grad = (
        (
            jnp.einsum(
                "bhlk,blhe->bkhe",
                cap_dscores,
                split_heads(cap_queries),
                preferred_element_type=jnp.float32,
            )
            * scale
        )
        .reshape(cap_items, cap_here, head_width)
        .astype(jnp.bfloat16)
    )
    caption_value_grad = (
        jnp.einsum("bhlk,blhe->bkhe", cap_low, cap_d_att, preferred_element_type=jnp.float32)
        .reshape(cap_items, cap_here, head_width)
        .astype(jnp.bfloat16)
    )
    grad_query = jnp.einsum("bld,ble->de", lat_norm, d_queries, preferred_element_type=jnp.float32)
    d_lat_norm = lax.psum(
        jnp.einsum("ble,de->bld", d_queries, query_weight, preferred_element_type=jnp.float32),
        "head",
    )
    d_lat_back, grad_gain_latent = norm_back(lat_float, gain_latent, d_lat_norm)
    latent_grad = d_after + d_lat_back
    grad_key = jnp.einsum(
        "zsg,zsv->gv", video_normed, video_key_grad, preferred_element_type=jnp.float32
    ) + jnp.einsum(
        "zsg,zsv->gv", caption_normed, caption_key_grad, preferred_element_type=jnp.float32
    )
    grad_value = jnp.einsum(
        "zsg,zsv->gv", video_normed, video_value_grad, preferred_element_type=jnp.float32
    ) + jnp.einsum(
        "zsg,zsv->gv", caption_normed, caption_value_grad, preferred_element_type=jnp.float32
    )
    video_term = jnp.einsum(
        "ayt,ot->ayo", video_key_grad, key_matrix, preferred_element_type=jnp.float32
    ) + jnp.einsum(
        "ayt,ot->ayo", video_value_grad, value_matrix, preferred_element_type=jnp.float32
    )
    cap_term = jnp.einsum(
        "ayt,ot->ayo", caption_key_grad, key_matrix, preferred_element_type=jnp.float32
    ) + jnp.einsum(
        "ayt,ot->ayo", caption_value_grad, value_matrix, preferred_element_type=jnp.float32
    )
    d_video_norm, d_cap_norm = lax.psum((video_term, cap_term), "head")
    video_grad, video_gain_part = norm_back(video_float, gain_tokens, d_video_norm)
    caption_grad, cap_gain_part = norm_back(cap_float, gain_tokens, d_cap_norm)
    grad_gain_tokens = video_gain_part + cap_gain_part
    kept_here = jnp.sum(keep)
    (
        grad_query,
        grad_key,
        grad_value,
        grad_out,
        grad_up,
        grad_down,
        grad_gain_latent,
        grad_gain_tokens,
        grad_gain_mlp,
        kept_total,
    ) = lax.psum(
        (
            grad_query,
            grad_key,
            grad_value,
            grad_out,
            grad_up,
            grad_down,
            grad_gain_latent,
            grad_gain_tokens,
            grad_gain_mlp,
            kept_here,
        ),
        ("vid", "txt"),
    )
    kept_count = (kept_total / vid_count).astype(jnp.int32)
    return (
        latents_out,
        latent_grad,
        video_grad,
        caption_grad,
        grad_query,
        grad_key,
        grad_value,
        grad_out,
        grad_up,
        grad_down,
        grad_gain_latent,
        grad_gain_tokens,
        grad_gain_mlp,
        kept_count,
    )


def solution(mesh):
    in_specs = (
        P("txt", "vid", None),
        P("txt", "vid", None),
        P("vid", "txt", None),
        P("vid"),
        P("vid", "txt"),
        P("txt"),
        P(),
        P(),
        P(),
        P(None, "head"),
        P(None, "head"),
        P(None, "head"),
        P("head", None),
        P(None, "head"),
        P("head", None),
        P("txt", "vid", None),
    )
    out_specs = (
        P("txt", "vid", None),
        P("txt", "vid", None),
        P("txt", "vid", None),
        P("vid", "txt", None),
        P(None, "head"),
        P(None, "head"),
        P(None, "head"),
        P("head", None),
        P(None, "head"),
        P("head", None),
        P(),
        P(),
        P(),
        P(),
    )
    return jax.shard_map(local, mesh=mesh, in_specs=in_specs, out_specs=out_specs, check_vma=False)
```

profile of v0, /device:TPU:0, one launch (start us, length us, event | category | flops | bytes accessed | tf_op | source)
XLA Modules:
  0.0 1152.1 jit_solution(121106021653798068)
XLA Ops:
  7.3 1.4 convert_reduce_fusion.1
  8.8 1.5 fusion.24
  13.7 3.7 convert_reduce_fusion
  19.3 4.8 fusion.13
  24.2 5.8 convolution_convert_fusion.1
  30.0 4.2 convolution_convert_fusion.2
  34.3 9.0 all-gather.5.cloned.1.call-done
  43.3 1.7 copy.105
  46.9 1.6 copy.107
  48.5 1.6 copy.106
  50.1 2.7 multiply_reduce_fusion.1
  52.8 1.6 exponential_reduce_fusion
  57.6 24.3 %all_gather.25 = f32[8,32,3,128]{3,1,2,0:T(8,128)S(1)} all-gather(f32[1,32,3,128]{3,1,2,0:T(8,128)S(1)} %copy.109), channel_id=1, replica_groups=mesh['vid'=2,'txt'=4,'head'=4] {'vid','txt'}, dimensions={0}, use_global_device_ids=true | all-gather | bytes 442368 | tf_op jit(solution)/shard_map/all_gather | solution.py:12
  81.9 24.3 %all_gather.28 = f32[8,32,3,128]{3,1,2,0:T(8,128)S(1)} all-gather(f32[1,32,3,128]{3,1,2,0:T(8,128)S(1)} %copy.110), channel_id=1, replica_groups=mesh['vid'=2,'txt'=4,'head'=4] {'vid','txt'}, dimensions={0}, use_global_device_ids=true | all-gather | bytes 442368 | tf_op jit(solution)/shard_map/all_gather | solution.py:12
  108.2 4.3 fusion.33
  112.5 1.4 copy.115
  113.9 1.6 fusion.86
  115.5 1.8 copy.117
  118.6 1.5 copy-done.17
  120.6 2.3 copy.118
  123.5 51.8 %reduce-scatter.3.cloned.1.call-done = f32[1,8,64,192]{3,2,1,0:T(8,128)} async-done(((f32[8,8,64,192]{3,2,1,0:T(8,128)}), f32[1,8,64,192]{3,2,1,0:T(8,128)}) %reduce-scatter.3.cloned.1.call-update) | async-done | bytes 393232 | tf_op jit(solution)/shard_map/reduce_scatter | solution.py:195
  175.3 2.6 fusion.67
  178.0 69.3 %all-reduce.9.cloned.1.call-done = f32[8,64,768]{2,1,0:T(8,128)} async-done(((f32[8,64,768]{2,1,0:T(8,128)}), f32[8,64,768]{2,1,0:T(8,128)}) %all-reduce.9.cloned.1.call-update) | async-done | bytes 1572880 | tf_op jit(solution)/shard_map/psum | solution.py:199
  247.3 1.6 fusion.118
  251.2 4.2 multiply_convert_fusion.2
  257.5 2.0 fusion.41
  260.6 3.0 convolution_convert_fusion.3
  263.7 64.1 %all-reduce.13.cloned.1.call-done = f32[8,64,768]{2,1,0:T(8,128)} async-done(((f32[8,64,768]{2,1,0:T(8,128)}), f32[8,64,768]{2,1,0:T(8,128)}) %all-reduce.13.cloned.1.call-update) | async-done | bytes 1572880 | tf_op jit(solution)/shard_map/psum | solution.py:217
  327.8 2.6 multiply_reduce_fusion.2
  330.4 43.3 %all-reduce.11.cloned.1.call-done = bf16[8,64,768]{2,1,0:T(8,128)(2,1)} async-done(((bf16[8,64,768]{2,1,0:T(8,128)(2,1)}), bf16[8,64,768]{2,1,0:T(8,128)(2,1)}) %all-reduce.11.cloned.1.call-update) | async-done | bytes 786448 | tf_op jit(solution)/shard_map/psum | solution.py:206
  373.6 3.1 fusion.116
  379.3 26.9 %all-gather.7.cloned.1.call-done = bf16[64,64,192]{2,1,0:T(8,128)(2,1)} async-done(((bf16[8,64,192]{2,1,0:T(8,128)(2,1)}), bf16[64,64,192]{2,1,0:T(8,128)(2,1)}) %all-gather.7.cloned.1.call-update) | async-done | bytes 1572880 | tf_op jit(solution)/shard_map/all_gather | solution.py:229
  406.2 1.7 copy.119
  410.6 5.8 multiply_reduce_fusion
  416.5 27.9 %psum.122 = f32[32,3,128]{2,1,0:T(4,128)S(1)} all-reduce(f32[32,3,128]{2,1,0:T(4,128)S(1)} %add_dynamic-update-slice_fusion.2), channel_id=1, replica_groups=mesh['vid'=2,'txt'=4,'head'=4] {'vid','txt'}, use_global_device_ids=true, to_apply=%region_22.23 | all-reduce | flops 12288 | bytes 98304 | tf_op jit(solution)/shard_map/psum | solution.py:245
  444.5 5.9 multiply_convert_fusion
  452.1 1.3 copy.123
  453.6 1.6 convolution_multiply_fusion
  455.2 1.8 copy.125
  458.8 2.3 copy.126
  467.9 1.9 fusion.71
  470.4 2.1 convolution_convert_fusion
  473.7 6.7 convolution_add_fusion
  480.4 32.0 %reduce-scatter.5.cloned.1.call-done = f32[1,8,64,192]{3,2,1,0:T(8,128)} async-done(((f32[8,8,64,192]{3,2,1,0:T(8,128)}), f32[1,8,64,192]{3,2,1,0:T(8,128)}) %reduce-scatter.5.cloned.1.call-update) | async-done | bytes 393232 | tf_op jit(solution)/shard_map/reduce_scatter | solution.py:272
  512.4 2.5 fusion.75
  516.2 3.5 convolution_bitcast_fusion
  519.8 2.5 convolution_bitcast_fusion.1
  522.4 1.3 convolution_bitcast_fusion.6
  524.2 2.6 convolution_bitcast_fusion.2
  528.4 2.6 convolution_bitcast_fusion.3
  532.3 1.3 convolution_bitcast_fusion.7
  533.7 484.3 %all-reduce.17.cloned.1.call-done = (f32[8,64,768]{2,1,0:T(8,128)}, f32[8,512,768]{2,1,0:T(8,128)}, f32[16,16,768]{2,1,0:T(8,128)}) async-done(((f32[8,64,768]{2,1,0:T(8,128)}, f32[8,512,768]{2,1,0:T(8,128)}, f32[16,16,768]{2,1,0:T(8,128)}), (f32[8,64,768]{2,1,0:T(8,128)}, f32[8,512,768]{2,1,0:T(8,128)}, f32[16,16,768]{2,1,0:T(8,128)})) %all-reduce.17.cloned.1.call-update) | async-done | bytes 14942224 | tf_op jit(solution)/shard_map/psum | solution.py:312
  1018.0 1.4 fusion.58
  1019.4 10.0 fusion.14
  1029.5 2.6 copy-done.2
  1032.1 6.6 fusion.12
  1040.6 28.1 %all-reduce = (f32[768]{0:T(1024)}, f32[768]{0:T(1024)}, f32[768]{0:T(1024)}, f32[]{:T(128)}) all-reduce(f32[768]{0:T(1024)S(1)} %get-tuple-element.163, f32[768]{0:T(1024)S(1)} %add.231, f32[768]{0:T(1024)S(1)} %copy-done.101, f32[]{:T(128)} %fusion.104), channel_id=1, replica_groups=mesh['vid'=2,'txt'=4,'head'=4] {'vid','txt'}, use_global_device_ids=true, to_apply=%region_40.41 | all-reduce | flops 2305 | bytes 18440 | tf_op jit(solution)/shard_map/psum | solution.py:354
  1069.4 2.4 broadcast_add_fusion.1
  1071.9 3.5 add_add_fusion.3
  1075.4 10.8 broadcast_add_fusion
  1086.2 49.6 %all-reduce.15.cloned.1.call-done = (f32[768,192]{0,1:T(8,128)}, f32[768,192]{0,1:T(8,128)}, f32[768,192]{0,1:T(8,128)}, f32[192,768]{1,0:T(8,128)}, f32[768,768]{1,0:T(8,128)}, /*index=5*/f32[768,768]{1,0:T(8,128)}) async-done(((f32[768,192]{0,1:T(8,128)}, f32[768,192]{0,1:T(8,128)}, f32[768,192]{0,1:T(8,128)}, f32[192,768]{1,0:T(8,128)}, f32[768,768]{1,0:T(8,128)}, /*index=5*/f32[768,768]{1,0:T(8,128)}), ...) | async-done | bytes 7077904 | tf_op jit(solution)/shard_map/psum | solution.py:354
  1135.8 2.0 copy.191
  1140.3 1.4 copy.195
  1142.8 1.4 copy.196
  (374 shorter events, 48.5 us)
Async XLA Ops:
  7.2 242.9 %copy-start = (bf16[768,768]{1,0:T(8,128)(2,1)S(1)}, bf16[768,768]{1,0:T(8,128)(2,1)}, u32[]{:S(2)}) copy-start(bf16[768,768]{1,0:T(8,128)(2,1)} %param.31) | copy-start | bytes 3538948
  7.2 4.2 copy-start.4
  7.2 4.2 copy-start.88
  7.2 4.2 copy-start.59
  7.2 36.0 %all-gather.5.cloned.1.call-start = ((), (), s32[]{:S(2)}) async-start(), calls=%async_computation.7 | async-start | bytes 2359296 | tf_op jit(solution)/shard_map/all_gather | solution.py:124
  12.6 162.7 %reduce-scatter.3.cloned.1.call-start = ((), (), s32[]{:S(2)}) async-start(), calls=%async_computation.2 | async-start | bytes 4718592 | tf_op jit(solution)/shard_map/reduce_scatter | solution.py:195
  12.8 5.0 copy-start.53
  13.7 4.2 copy-start.65
  13.7 3.8 copy-start.40
  13.7 3.8 copy-start.63
  13.7 4.2 copy-start.38
  19.1 36.4 %copy-start.32 = (bf16[16,16,3,64]{3,2,1,0:T(4,128)(2,1)}, bf16[16,16,3,64]{3,2,1,0:T(4,128)(2,1)S(1)}, u32[]{:S(2)}) copy-start(bf16[16,16,3,64]{3,2,1,0:T(4,128)(2,1)S(1)} %reshape.239) | copy-start | bytes 294916
  19.3 36.3 %copy-start.84 = (pred[16,16]{1,0:T(8,128)(4,1)}, pred[16,16]{1,0:T(8,128)(4,1)S(1)}, u32[]{:S(2)}) copy-start(pred[16,16]{1,0:T(8,128)(4,1)S(1)} %compare_and_fusion) | copy-start | bytes 772
  19.3 10.8 slice-start
  24.1 5.9 copy-start.67
  24.1 5.9 copy-start.69
  24.2 5.9 slice-start.1
  48.5 7.1 copy-start.18
  50.1 2.7 copy-start.26
  52.8 2.7 copy-start.3
  107.5 5.0 copy-start.75
  107.5 5.0 copy-start.78
  122.9 52.5 %copy-start.61 = (bf16[192,768]{1,0:T(8,128)(2,1)S(1)}, bf16[192,768]{1,0:T(8,128)(2,1)}, u32[]{:S(2)}) copy-start(bf16[192,768]{1,0:T(8,128)(2,1)} %param.30) | copy-start | bytes 884740
  122.9 124.4 %all-reduce.9.cloned.1.call-start = ((), (), s32[]{:S(2)}) async-start(), calls=%async_computation.3 | async-start | bytes 3145728 | tf_op jit(solution)/shard_map/psum | solution.py:199
  123.5 54.4 %copy-start.107 = (f32[8]{0:T(128)}, f32[8]{0:T(128)S(1)}, u32[]{:S(2)}) copy-start(f32[8]{0:T(128)S(1)} %subtract_convert_fusion) | copy-start | bytes 100
  178.0 149.8 %all-reduce.13.cloned.1.call-start = ((), (), s32[]{:S(2)}) async-start(), calls=%async_computation.5 | async-start | bytes 3145728 | tf_op jit(solution)/shard_map/psum | solution.py:217
  248.9 124.7 %copy-start.8 = (f32[8,64,768]{2,1,0:T(8,128)}, f32[8,64,768]{2,1,0:T(8,128)S(1)}, u32[]{:S(2)}) copy-start(f32[8,64,768]{2,1,0:T(8,128)S(1)} %get-tuple-element.199) | copy-start | bytes 4718596
  251.2 4.3 copy-start.28
  251.2 4.3 copy-start.110
  259.5 114.1 %all-reduce.11.cloned.1.call-start = ((), (), s32[]{:S(2)}) async-start(), calls=%async_computation.4 | async-start | bytes 1572864 | tf_op jit(solution)/shard_map/psum | solution.py:206
  260.6 67.2 %copy-start.82 = (f32[8,64]{1,0:T(8,128)S(1)}, f32[8,64]{1,0:T(8,128)}, u32[]{:S(2)}) copy-start(f32[8,64]{1,0:T(8,128)} %copy-done.81) | copy-start | bytes 6148
  260.6 67.2 %copy-start.99 = (f32[8,64]{1,0:T(8,128)S(1)}, f32[8,64]{1,0:T(8,128)}, u32[]{:S(2)}) copy-start(f32[8,64]{1,0:T(8,128)} %copy-done.98) | copy-start | bytes 6148
  260.6 67.2 %copy-start.103 = (f32[768]{0:T(1024)S(1)}, f32[768]{0:T(1024)}, u32[]{:S(2)}) copy-start(f32[768]{0:T(1024)} %param.26) | copy-start | bytes 9220
  263.6 66.7 %copy-start.97 = (f32[8,64]{1,0:T(8,128)S(1)}, f32[8,64]{1,0:T(8,128)}, u32[]{:S(2)}) copy-start(f32[8,64]{1,0:T(8,128)} %copy-done.96) | copy-start | bytes 6148
  263.6 142.5 %all-gather.7.cloned.1.call-start = ((), (), s32[]{:S(2)}) async-start(), calls=%async_computation.8 | async-start | bytes 2359296 | tf_op jit(solution)/shard_map/all_gather | solution.py:229
  377.9 30.0 %copy-start.45 = (bf16[8,64,768]{2,1,0:T(8,128)(2,1)}, bf16[8,64,768]{2,1,0:T(8,128)(2,1)S(1)}, u32[]{:S(2)}) copy-start(bf16[8,64,768]{2,1,0:T(8,128)(2,1)S(1)} %fusion.48) | copy-start | bytes 2359300
  379.0 133.4 %reduce-scatter.5.cloned.1.call-start = ((), (), s32[]{:S(2)}) async-start(), calls=%async_computation.6 | async-start | bytes 4718592 | tf_op jit(solution)/shard_map/reduce_scatter | solution.py:272
  409.0 7.4 copy-start.55
  444.5 6.0 copy-start.23
  461.1 557.0 %all-reduce.17.cloned.1.call-start = ((), (), s32[]{:S(2)}) async-start(), calls=%async_computation.10 | async-start | bytes 29884416 | tf_op jit(solution)/shard_map/psum | solution.py:312
  466.2 3.6 slice-start.8
  473.7 38.7 %copy-start.60 = (bf16[768,192]{0,1:T(8,128)(2,1)S(1)}, bf16[768,192]{0,1:T(8,128)(2,1)}, u32[]{:S(2)}) copy-start(bf16[768,192]{0,1:T(8,128)(2,1)} %param.27) | copy-start | bytes 884740
  514.9 8.7 slice-start.2
  514.9 620.9 %all-reduce.15.cloned.1.call-start = ((), (), s32[]{:S(2)}) async-start(), calls=%async_computation.9 | async-start | bytes 14155776 | tf_op jit(solution)/shard_map/psum | solution.py:354
  516.2 3.5 copy-start.9
  516.2 3.5 copy-start.83
  516.2 3.5 copy-start.100
  516.2 3.5 copy-start.104
  516.2 3.5 copy-start.115
  516.2 7.4 slice-start.3
  524.2 2.7 copy-start.37
  533.7 495.8 %slice-start.4 = ((s8[6291456]{0:T(1024)(128)(4,1)}), s8[2097152]{0:T(1024)(128)(4,1)S(1)}, s32[]{:S(2)}) async-start(s8[6291456]{0:T(1024)(128)(4,1)} %bitcast.180), calls=%async_computation.15 | async-start | bytes 4194304
  1019.4 10.0 copy-start.68
  1019.4 10.1 slice-start.5
  1019.4 12.7 %copy-start.2 = (f32[8,512,768]{2,1,0:T(8,128)S(1)}, f32[8,512,768]{2,1,0:T(8,128)}, u32[]{:S(2)}) copy-start(f32[8,512,768]{2,1,0:T(8,128)} %get-tuple-element.190) | copy-start | bytes 37748740
  1032.1 6.6 copy-start.74
  1032.1 6.6 copy-start.20
  1032.1 7.1 copy-start.14
  1039.2 36.1 %slice-start.6 = ((s8[6291456]{0:T(1024)(128)(4,1)}), s8[2097152]{0:T(1024)(128)(4,1)S(1)}, s32[]{:S(2)}) async-start(s8[6291456]{0:T(1024)(128)(4,1)} %bitcast.182), calls=%async_computation.17 | async-start | bytes 4194304
  1040.6 31.3 %copy-start.93 = (f32[8,64]{1,0:T(8,128)S(1)}, f32[8,64]{1,0:T(8,128)}, u32[]{:S(2)}) copy-start(f32[8,64]{1,0:T(8,128)} %copy-done.92) | copy-start | bytes 6148
  1069.4 5.9 slice-start.7
  1135.8 2.9 copy-start.49
  1135.8 3.7 copy-start.48
  1140.3 3.9 copy-start.1
  (71 other events, 106.4 us)
Sparse Core Ops, SparseCore 0:
  12.7 30.4 all-gather.4
  123.0 52.2 reduce-scatter.2
  178.3 68.9 all-reduce.8
  259.6 68.1 all-reduce.12
  330.6 42.9 all-reduce.10
  379.1 27.0 all-gather.6
  461.2 51.1 reduce-scatter.4
  515.8 502.2 all-reduce.16
  1023.3 112.5 all-reduce.14
where the time goes:
time: 1160 us; the launch traced here: 1150 us
  waiting for transfers between devices  830 us (72%)
  blocking collectives  105 us (9%)
  matrix products  73.1 us (6%)
  other arithmetic  71.8 us (6%)
  local copies, waits for them, and re-layouts  53.3 us (5%)
  between operations  17.4 us (1%)
    psum x1, waiting for transfers between devices, local(): lax.psum(jnp.einsum('ble,de->bld', d_queries, query_weight, preferred_ele...  484 us
    psum x1, waiting for transfers between devices, local(): lax.psum(jnp.einsum('ble,ed->bld', mixed_in, out_weight, preferred_elemen...  69.3 us
    psum x1, waiting for transfers between devices, local(): lax.psum(jnp.einsum('blf,df->bld', d_pre, up_weight, preferred_element_ty...  64.1 us
    reduce_scatter x1, waiting for transfers between devices, local(): lax.psum_scatter(to_blocks(value_all, vid_count, txt_count), ('vid', 'txt...  51.8 us
    psum x1, waiting for transfers between devices, local(): lax.psum((grad_query, grad_key, grad_value, grad_out, grad_up, grad_down,...  49.6 us
    all_gather x2, blocking collectives, combined_all(): gathered = jax.tree.map(lambda a: lax.all_gather(a, axis), part)  48.6 us
    psum x1, waiting for transfers between devices, local(): lax.psum(jnp.einsum('blf,fd->bld', activ, down_weight, preferred_element_...  43.3 us
    reduce_scatter x1, waiting for transfers between devices, local(): lax.psum_scatter(to_blocks(query_all, vid_count, txt_count), ('vid', 'txt...  32 us
  transfers between devices with their start and end apart: 9, of which 9 were waited for; matrix products, arithmetic and copies ran while one was open for 8% of the time, Pallas kernels for 0%

commit v1 on v0

--- a/solution.py
+++ b/solution.py
@@ -196,8 +196,12 @@
         to_blocks(value_all, vid_count, txt_count), ("vid", "txt"), scatter_dimension=0, tiled=True
     )[0]
     mixed_in = (attended * keep[:, None, None]).astype(jnp.bfloat16)
-    branch = lax.psum(
-        jnp.einsum("ble,ed->bld", mixed_in, out_weight, preferred_element_type=jnp.float32), "head"
+    branch = jnp.sum(
+        lax.all_gather(
+            jnp.einsum("ble,ed->bld", mixed_in, out_weight, preferred_element_type=jnp.float32),
+            "head",
+        ),
+        axis=0,
     )
     after_attn = lat_float + branch
     mlp_norm = layer_norm(after_attn, gain_mlp).astype(jnp.bfloat16)

time: 1160 us -> 1210 us (1.043)
  waiting for transfers between devices: 830 us -> 876 us
    all_gather x0 -> x1, waiting for transfers between devices: none -> 115 us  [local(): lax.all_gather(jnp.einsum('ble,ed->bld', mixed_in, out_weight, preferred_...]
    psum x1 -> x0, waiting for transfers between devices: 69.3 us -> none  [local(): lax.psum(jnp.einsum('ble,ed->bld', mixed_in, out_weight, preferred_elemen...]
where the time goes in v1:
time: 1210 us; the launch traced here: 1200 us
  waiting for transfers between devices  876 us (72%)
  blocking collectives  105 us (9%)
  other arithmetic  76.3 us (6%)
  matrix products  73.1 us (6%)
  local copies, waits for them, and re-layouts  53.3 us (4%)
  between operations  17.4 us (1%)
    psum x1, waiting for transfers between devices, local(): lax.psum(jnp.einsum('ble,de->bld', d_queries, query_weight, preferred_ele...  484 us
    all_gather x1, waiting for transfers between devices, local(): lax.all_gather(jnp.einsum('ble,ed->bld', mixed_in, out_weight, preferred_...  115 us
    psum x1, waiting for transfers between devices, local(): lax.psum(jnp.einsum('blf,df->bld', d_pre, up_weight, preferred_element_ty...  63.1 us
    reduce_scatter x1, waiting for transfers between devices, local(): lax.psum_scatter(to_blocks(value_all, vid_count, txt_count), ('vid', 'txt...  51.8 us
    psum x1, waiting for transfers between devices, local(): lax.psum((grad_query, grad_key, grad_value, grad_out, grad_up, grad_down,...  49.6 us
    all_gather x2, blocking collectives, combined_all(): gathered = jax.tree.map(lambda a: lax.all_gather(a, axis), part)  48.6 us
    psum x1, waiting for transfers between devices, local(): lax.psum(jnp.einsum('blf,fd->bld', activ, down_weight, preferred_element_...  43.3 us
    reduce_scatter x1, waiting for transfers between devices, local(): lax.psum_scatter(to_blocks(query_all, vid_count, txt_count), ('vid', 'txt...  32 us
  transfers between devices with their start and end apart: 9, of which 9 were waited for; matrix products, arithmetic and copies ran while one was open for 8% of the time, Pallas kernels for 0%

profile of v1, /device:TPU:0, one launch (start us, length us, event | category | flops | bytes accessed | tf_op | source)
XLA Modules:
  0.0 1201.8 jit_solution(16902197407053476876)
XLA Ops:
  7.3 1.4 convert_reduce_fusion.1
  8.8 1.5 fusion.24
  13.7 3.7 convert_reduce_fusion
  19.3 4.8 fusion.13
  24.2 5.8 convolution_convert_fusion.1
  30.0 4.2 convolution_convert_fusion.2
  34.3 9.0 all-gather.7.cloned.1.call-done
  43.3 1.7 copy.105
  46.9 1.6 copy.107
  48.5 1.6 copy.106
  50.1 2.7 multiply_reduce_fusion.1
  52.8 1.6 exponential_reduce_fusion
  57.6 24.3 %all_gather.31 = f32[8,32,3,128]{3,1,2,0:T(8,128)S(1)} all-gather(f32[1,32,3,128]{3,1,2,0:T(8,128)S(1)} %copy.109), channel_id=1, replica_groups=mesh['vid'=2,'txt'=4,'head'=4] {'vid','txt'}, dimensions={0}, use_global_device_ids=true | all-gather | bytes 442368 | tf_op jit(solution)/shard_map/all_gather | solution.py:12
  81.9 24.3 %all_gather.34 = f32[8,32,3,128]{3,1,2,0:T(8,128)S(1)} all-gather(f32[1,32,3,128]{3,1,2,0:T(8,128)S(1)} %copy.110), channel_id=1, replica_groups=mesh['vid'=2,'txt'=4,'head'=4] {'vid','txt'}, dimensions={0}, use_global_device_ids=true | all-gather | bytes 442368 | tf_op jit(solution)/shard_map/all_gather | solution.py:12
  108.2 4.3 fusion.33
  112.5 1.4 copy.115
  113.9 1.6 fusion.86
  115.5 1.8 copy.117
  118.6 1.5 copy-done.17
  120.6 2.3 copy.118
  123.5 51.8 %reduce-scatter.3.cloned.1.call-done = f32[1,8,64,192]{3,2,1,0:T(8,128)} async-done(((f32[8,8,64,192]{3,2,1,0:T(8,128)}), f32[1,8,64,192]{3,2,1,0:T(8,128)}) %reduce-scatter.3.cloned.1.call-update) | async-done | bytes 393232 | tf_op jit(solution)/shard_map/reduce_scatter | solution.py:195
  175.3 2.6 fusion.67
  178.0 115.4 %all-gather.9.cloned.1.call-done = f32[32,64,768]{2,1,0:T(8,128)} async-done(((f32[8,64,768]{2,1,0:T(8,128)}), f32[32,64,768]{2,1,0:T(8,128)}) %all-gather.9.cloned.1.call-update) | async-done | bytes 6291472 | tf_op jit(solution)/shard_map/all_gather | solution.py:200
  293.4 4.5 reduce_sum.240
  297.9 1.6 fusion.118
  301.8 4.2 multiply_convert_fusion.2
  308.2 2.0 fusion.41
  311.3 3.0 convolution_convert_fusion.3
  314.3 63.1 %all-reduce.10.cloned.1.call-done = f32[8,64,768]{2,1,0:T(8,128)} async-done(((f32[8,64,768]{2,1,0:T(8,128)}), f32[8,64,768]{2,1,0:T(8,128)}) %all-reduce.10.cloned.1.call-update) | async-done | bytes 1572880 | tf_op jit(solution)/shard_map/psum | solution.py:221
  377.5 2.6 multiply_reduce_fusion.2
  380.0 43.3 %all-reduce.8.cloned.1.call-done = bf16[8,64,768]{2,1,0:T(8,128)(2,1)} async-done(((bf16[8,64,768]{2,1,0:T(8,128)(2,1)}), bf16[8,64,768]{2,1,0:T(8,128)(2,1)}) %all-reduce.8.cloned.1.call-update) | async-done | bytes 786448 | tf_op jit(solution)/shard_map/psum | solution.py:210
  423.3 3.1 fusion.116
  428.9 26.9 %all-gather.11.cloned.1.call-done = bf16[64,64,192]{2,1,0:T(8,128)(2,1)} async-done(((bf16[8,64,192]{2,1,0:T(8,128)(2,1)}), bf16[64,64,192]{2,1,0:T(8,128)(2,1)}) %all-gather.11.cloned.1.call-update) | async-done | bytes 1572880 | tf_op jit(solution)/shard_map/all_gather | solution.py:233
  455.9 1.7 copy.119
  460.3 5.8 multiply_reduce_fusion
  466.2 27.9 %psum.114 = f32[32,3,128]{2,1,0:T(4,128)S(1)} all-reduce(f32[32,3,128]{2,1,0:T(4,128)S(1)} %add_dynamic-update-slice_fusion.2), channel_id=1, replica_groups=mesh['vid'=2,'txt'=4,'head'=4] {'vid','txt'}, use_global_device_ids=true, to_apply=%region_22.23 | all-reduce | flops 12288 | bytes 98304 | tf_op jit(solution)/shard_map/psum | solution.py:249
  494.2 5.9 multiply_convert_fusion
  501.8 1.3 copy.123
  503.3 1.6 convolution_multiply_fusion
  504.8 1.8 copy.125
  508.4 2.3 copy.126
  517.6 1.9 fusion.71
  520.1 2.1 convolution_convert_fusion
  523.3 6.7 convolution_add_fusion
  530.1 32.0 %reduce-scatter.5.cloned.1.call-done = f32[1,8,64,192]{3,2,1,0:T(8,128)} async-done(((f32[8,8,64,192]{3,2,1,0:T(8,128)}), f32[1,8,64,192]{3,2,1,0:T(8,128)}) %reduce-scatter.5.cloned.1.call-update) | async-done | bytes 393232 | tf_op jit(solution)/shard_map/reduce_scatter | solution.py:276
  562.0 2.5 fusion.75
  565.9 3.5 convolution_bitcast_fusion
  569.5 2.5 convolution_bitcast_fusion.1
  573.9 2.6 convolution_bitcast_fusion.2
  578.1 2.6 convolution_bitcast_fusion.3
  582.0 1.3 convolution_bitcast_fusion.7
  583.4 484.3 %all-reduce.14.cloned.1.call-done = (f32[8,64,768]{2,1,0:T(8,128)}, f32[8,512,768]{2,1,0:T(8,128)}, f32[16,16,768]{2,1,0:T(8,128)}) async-done(((f32[8,64,768]{2,1,0:T(8,128)}, f32[8,512,768]{2,1,0:T(8,128)}, f32[16,16,768]{2,1,0:T(8,128)}), (f32[8,64,768]{2,1,0:T(8,128)}, f32[8,512,768]{2,1,0:T(8,128)}, f32[16,16,768]{2,1,0:T(8,128)})) %all-reduce.14.cloned.1.call-update) | async-done | bytes 14942224 | tf_op jit(solution)/shard_map/psum | solution.py:316
  1067.7 1.4 fusion.58
  1069.1 10.0 fusion.14
  1079.2 2.6 copy-done.2
  1081.8 6.6 fusion.12
  1090.3 28.1 %all-reduce = (f32[768]{0:T(1024)}, f32[768]{0:T(1024)}, f32[768]{0:T(1024)}, f32[]{:T(128)}) all-reduce(f32[768]{0:T(1024)S(1)} %get-tuple-element.163, f32[768]{0:T(1024)S(1)} %add.229, f32[768]{0:T(1024)S(1)} %copy-done.101, f32[]{:T(128)} %fusion.104), channel_id=1, replica_groups=mesh['vid'=2,'txt'=4,'head'=4] {'vid','txt'}, use_global_device_ids=true, to_apply=%region_40.41 | all-reduce | flops 2305 | bytes 18440 | tf_op jit(solution)/shard_map/psum | solution.py:358
  1119.1 2.4 broadcast_add_fusion.1
  1121.6 3.5 add_add_fusion.3
  1125.1 10.8 broadcast_add_fusion
  1135.9 49.6 %all-reduce.12.cloned.1.call-done = (f32[768,192]{0,1:T(8,128)}, f32[768,192]{0,1:T(8,128)}, f32[768,192]{0,1:T(8,128)}, f32[192,768]{1,0:T(8,128)}, f32[768,768]{1,0:T(8,128)}, /*index=5*/f32[768,768]{1,0:T(8,128)}) async-done(((f32[768,192]{0,1:T(8,128)}, f32[768,192]{0,1:T(8,128)}, f32[768,192]{0,1:T(8,128)}, f32[192,768]{1,0:T(8,128)}, f32[768,768]{1,0:T(8,128)}, /*index=5*/f32[768,768]{1,0:T(8,128)}), ...) | async-done | bytes 7077904 | tf_op jit(solution)/shard_map/psum | solution.py:358
  1185.5 2.0 copy.191
  1190.0 1.4 copy.195
  1192.5 1.4 copy.196
  (375 shorter events, 49.7 us)
Async XLA Ops:
  7.2 293.5 %copy-start = (bf16[768,768]{1,0:T(8,128)(2,1)S(1)}, bf16[768,768]{1,0:T(8,128)(2,1)}, u32[]{:S(2)}) copy-start(bf16[768,768]{1,0:T(8,128)(2,1)} %param.31) | copy-start | bytes 3538948
  7.2 4.2 copy-start.4
  7.2 4.2 copy-start.88
  7.2 4.2 copy-start.59
  7.2 36.0 %all-gather.7.cloned.1.call-start = ((), (), s32[]{:S(2)}) async-start(), calls=%async_computation.6 | async-start | bytes 2359296 | tf_op jit(solution)/shard_map/all_gather | solution.py:124
  12.6 162.7 %reduce-scatter.3.cloned.1.call-start = ((), (), s32[]{:S(2)}) async-start(), calls=%async_computation.2 | async-start | bytes 4718592 | tf_op jit(solution)/shard_map/reduce_scatter | solution.py:195
  12.8 5.0 copy-start.53
  13.7 4.2 copy-start.65
  13.7 3.8 copy-start.40
  13.7 3.8 copy-start.63
  13.7 4.2 copy-start.38
  19.1 36.4 %copy-start.32 = (bf16[16,16,3,64]{3,2,1,0:T(4,128)(2,1)}, bf16[16,16,3,64]{3,2,1,0:T(4,128)(2,1)S(1)}, u32[]{:S(2)}) copy-start(bf16[16,16,3,64]{3,2,1,0:T(4,128)(2,1)S(1)} %reshape.239) | copy-start | bytes 294916
  19.3 36.3 %copy-start.84 = (pred[16,16]{1,0:T(8,128)(4,1)}, pred[16,16]{1,0:T(8,128)(4,1)S(1)}, u32[]{:S(2)}) copy-start(pred[16,16]{1,0:T(8,128)(4,1)S(1)} %compare_and_fusion) | copy-start | bytes 772
  19.3 10.8 slice-start
  24.1 5.9 copy-start.67
  24.1 5.9 copy-start.69
  24.2 5.9 slice-start.1
  48.5 7.1 copy-start.18
  50.1 2.7 copy-start.26
  52.8 2.7 copy-start.3
  107.5 5.0 copy-start.75
  107.5 5.0 copy-start.78
  122.9 52.5 %copy-start.61 = (bf16[192,768]{1,0:T(8,128)(2,1)S(1)}, bf16[192,768]{1,0:T(8,128)(2,1)}, u32[]{:S(2)}) copy-start(bf16[192,768]{1,0:T(8,128)(2,1)} %param.30) | copy-start | bytes 884740
  122.9 170.5 %all-gather.9.cloned.1.call-start = ((), (), s32[]{:S(2)}) async-start(), calls=%async_computation.7 | async-start | bytes 7864320 | tf_op jit(solution)/shard_map/all_gather | solution.py:200
  123.5 54.4 %copy-start.107 = (f32[8]{0:T(128)}, f32[8]{0:T(128)S(1)}, u32[]{:S(2)}) copy-start(f32[8]{0:T(128)S(1)} %subtract_convert_fusion) | copy-start | bytes 100
  178.0 199.5 %all-reduce.10.cloned.1.call-start = ((), (), s32[]{:S(2)}) async-start(), calls=%async_computation.4 | async-start | bytes 3145728 | tf_op jit(solution)/shard_map/psum | solution.py:221
  299.6 123.7 %copy-start.8 = (f32[8,64,768]{2,1,0:T(8,128)}, f32[8,64,768]{2,1,0:T(8,128)S(1)}, u32[]{:S(2)}) copy-start(f32[8,64,768]{2,1,0:T(8,128)S(1)} %get-tuple-element.199) | copy-start | bytes 4718596
  301.8 4.3 copy-start.28
  301.8 4.3 copy-start.110
  310.2 113.1 %all-reduce.8.cloned.1.call-start = ((), (), s32[]{:S(2)}) async-start(), calls=%async_computation.3 | async-start | bytes 1572864 | tf_op jit(solution)/shard_map/psum | solution.py:210
  311.3 66.2 %copy-start.82 = (f32[8,64]{1,0:T(8,128)S(1)}, f32[8,64]{1,0:T(8,128)}, u32[]{:S(2)}) copy-start(f32[8,64]{1,0:T(8,128)} %copy-done.81) | copy-start | bytes 6148
  311.3 66.2 %copy-start.99 = (f32[8,64]{1,0:T(8,128)S(1)}, f32[8,64]{1,0:T(8,128)}, u32[]{:S(2)}) copy-start(f32[8,64]{1,0:T(8,128)} %copy-done.98) | copy-start | bytes 6148
  311.3 66.2 %copy-start.103 = (f32[768]{0:T(1024)S(1)}, f32[768]{0:T(1024)}, u32[]{:S(2)}) copy-start(f32[768]{0:T(1024)} %param.26) | copy-start | bytes 9220
  314.3 65.8 %copy-start.97 = (f32[8,64]{1,0:T(8,128)S(1)}, f32[8,64]{1,0:T(8,128)}, u32[]{:S(2)}) copy-start(f32[8,64]{1,0:T(8,128)} %copy-done.96) | copy-start | bytes 6148
  314.3 141.6 %all-gather.11.cloned.1.call-start = ((), (), s32[]{:S(2)}) async-start(), calls=%async_computation.8 | async-start | bytes 2359296 | tf_op jit(solution)/shard_map/all_gather | solution.py:233
  427.6 30.0 %copy-start.45 = (bf16[8,64,768]{2,1,0:T(8,128)(2,1)}, bf16[8,64,768]{2,1,0:T(8,128)(2,1)S(1)}, u32[]{:S(2)}) copy-start(bf16[8,64,768]{2,1,0:T(8,128)(2,1)S(1)} %fusion.48) | copy-start | bytes 2359300
  428.7 133.4 %reduce-scatter.5.cloned.1.call-start = ((), (), s32[]{:S(2)}) async-start(), calls=%async_computation.5 | async-start | bytes 4718592 | tf_op jit(solution)/shard_map/reduce_scatter | solution.py:276
  458.7 7.4 copy-start.55
  494.1 6.0 copy-start.23
  510.7 557.0 %all-reduce.14.cloned.1.call-start = ((), (), s32[]{:S(2)}) async-start(), calls=%async_computation.10 | async-start | bytes 29884416 | tf_op jit(solution)/shard_map/psum | solution.py:316
  515.9 3.6 slice-start.8
  523.3 38.7 %copy-start.60 = (bf16[768,192]{0,1:T(8,128)(2,1)S(1)}, bf16[768,192]{0,1:T(8,128)(2,1)}, u32[]{:S(2)}) copy-start(bf16[768,192]{0,1:T(8,128)(2,1)} %param.27) | copy-start | bytes 884740
  564.6 8.7 slice-start.2
  564.6 620.9 %all-reduce.12.cloned.1.call-start = ((), (), s32[]{:S(2)}) async-start(), calls=%async_computation.9 | async-start | bytes 14155776 | tf_op jit(solution)/shard_map/psum | solution.py:358
  565.9 3.5 copy-start.9
  565.9 3.5 copy-start.83
  565.9 3.5 copy-start.100
  565.9 3.5 copy-start.104
  565.9 3.5 copy-start.115
  565.9 7.4 slice-start.3
  573.8 2.7 copy-start.37
  583.3 495.8 %slice-start.4 = ((s8[6291456]{0:T(1024)(128)(4,1)}), s8[2097152]{0:T(1024)(128)(4,1)S(1)}, s32[]{:S(2)}) async-start(s8[6291456]{0:T(1024)(128)(4,1)} %bitcast.181), calls=%async_computation.15 | async-start | bytes 4194304
  1069.1 10.0 copy-start.68
  1069.1 10.1 slice-start.5
  1069.1 12.7 %copy-start.2 = (f32[8,512,768]{2,1,0:T(8,128)S(1)}, f32[8,512,768]{2,1,0:T(8,128)}, u32[]{:S(2)}) copy-start(f32[8,512,768]{2,1,0:T(8,128)} %get-tuple-element.190) | copy-start | bytes 37748740
  1081.8 6.6 copy-start.74
  1081.8 6.6 copy-start.20
  1081.8 7.1 copy-start.14
  1088.9 36.1 %slice-start.6 = ((s8[6291456]{0:T(1024)(128)(4,1)}), s8[2097152]{0:T(1024)(128)(4,1)S(1)}, s32[]{:S(2)}) async-start(s8[6291456]{0:T(1024)(128)(4,1)} %bitcast.183), calls=%async_computation.17 | async-start | bytes 4194304
  1090.3 31.3 %copy-start.93 = (f32[8,64]{1,0:T(8,128)S(1)}, f32[8,64]{1,0:T(8,128)}, u32[]{:S(2)}) copy-start(f32[8,64]{1,0:T(8,128)} %copy-done.92) | copy-start | bytes 6148
  1119.1 5.9 slice-start.7
  1185.5 2.9 copy-start.49
  1185.5 3.7 copy-start.48
  1190.0 3.9 copy-start.1
  (71 other events, 106.4 us)
Sparse Core Ops, SparseCore 0:
  12.7 30.4 all-gather.6
  123.0 52.2 reduce-scatter.2
  178.1 115.3 all-gather.8
  310.3 67.1 all-reduce.9
  380.3 42.9 all-reduce.7
  428.8 27.0 all-gather.10
  510.9 51.1 reduce-scatter.4
  565.4 502.2 all-reduce.13
  1072.9 112.5 all-reduce.11
